TPU v7x, 32 devices: a whole 2x2x4 slice. The times are simulated.
32 devices in a mesh: sph: 8 (over z, x), ang: 4 (over y, core).
Axes of the slice: x: 2, y: 2, z: 4, core: 2. Of those that a mesh axis runs over, the one named last changes fastest.
Arguments:
- coefficients: bfloat16 [256, 240, 1024], P(('sph', 'ang')), may hold values from -0.039794922 to 0.039794922
- positions: int32 [256, 3], P(('sph', 'ang')), may hold values from 0 to 7
- shift_tables: bfloat16 [3, 8, 480, 240], replicated, may hold values from -1.3 to 1.3
- absorb_weight: float32 [256, 240], P(('sph', 'ang')), may hold values from 0.02 to 0.9, as said below
- incident: float32 [240, 1024], replicated, may hold values from -1.6 to 1.6
- detector: float32 [32, 64], P('sph'), may hold values from 0.002 to 0.18, as said below
Outputs:
- amplitude: float32 [2, 2, 32, 64, 512], P(None, None, 'sph', 'ang')
- cross_sections: float32 [3, 512], P(None, 'ang')
Inputs may be any that keep to these rules, and one draw needn't show every extreme that they name: `absorb_weight`: Positive. `detector`: Positive.
All inputs are finite; a program needn't handle non-finite values.
Results may differ from a plain program's by a relative error of at most 0.0003.
The roundings to bfloat16 on the way count: a program that leaves them out, or rounds other values in their place, can miss the bound.
Values sent between devices are 32-bit elements; how exact they have to be, the bound alone decides.
A program may use at most 128 MiB of HBM per device.

v0:
```python
import math
import jax
import jax.numpy as jnp
from jax import lax
from jax.sharding import PartitionSpec as P

ORDER = 10
AZIM = 64
POL_DEV = 4


def legendre_table(cos_theta, sine_theta, order):
    values = {}
    values[0, 0] = jnp.zeros_like(cos_theta) + 1.0 / math.sqrt(4.0 * math.pi)
    for azim_order in range(order + 1):
        if azim_order > 0:
            factor = -math.sqrt((2.0 * azim_order + 1.0) / (2.0 * azim_order))
            values[azim_order, azim_order] = (
                factor * sine_theta * values[azim_order - 1, azim_order - 1]
            )
        if azim_order + 1 <= order:
            values[azim_order + 1, azim_order] = (
                math.sqrt(2.0 * azim_order + 3.0) * cos_theta * values[azim_order, azim_order]
            )
        for degree in range(azim_order + 2, order + 1):
            upper_coef = math.sqrt(
                (4.0 * degree * degree - 1.0) / (degree * degree - azim_order * azim_order)
            )
            lower_coef = math.sqrt(
                ((degree - 1.0) * (degree - 1.0) - azim_order * azim_order)
                / (4.0 * (degree - 1.0) * (degree - 1.0) - 1.0)
            )
            values[degree, azim_order] = upper_coef * (
                cos_theta * values[degree - 1, azim_order]
                - lower_coef * values[degree - 2, azim_order]
            )
    return values


def angular_basis(polar_index, azim_index, polar_total, azim_total, order):
    theta = (polar_index.astype(jnp.float32) + 0.5) * (math.pi / polar_total)
    azimuth = azim_index.astype(jnp.float32) * (2.0 * math.pi / azim_total)
    cos_theta = jnp.cos(theta)
    sine_theta = jnp.sin(theta)
    legendre_values = legendre_table(cos_theta, sine_theta, order)
    pi_terms = []
    tau_terms = []
    orders_list = []
    phase_real = []
    phase_imag = []
    unit_powers = [(1.0, 0.0), (0.0, -1.0), (-1.0, 0.0), (0.0, 1.0)]
    for degree in range(1, order + 1):
        norm_factor = 1.0 / math.sqrt(degree * (degree + 1.0))
        power_real, power_imag = unit_powers[(degree + 1) % 4]
        for azim_order in range(-degree, degree + 1):
            size_m = abs(azim_order)
            current = legendre_values[degree, size_m]
            if degree - 1 >= size_m:
                previous = legendre_values[degree - 1, size_m]
            else:
                previous = jnp.zeros_like(current)
            link = math.sqrt(
                (2.0 * degree + 1.0)
                * (degree * degree - azim_order * azim_order)
                / (2.0 * degree - 1.0)
            )
            pi_terms.append(azim_order * current / sine_theta)
            tau_terms.append((degree * cos_theta * current - link * previous) / sine_theta)
            orders_list.append(float(azim_order))
            phase_real.append(power_real * norm_factor)
            phase_imag.append(power_imag * norm_factor)
    pi_block = jnp.stack(pi_terms, axis=1)[:, None, :]
    tau_block = jnp.stack(tau_terms, axis=1)[:, None, :]
    orders_row = jnp.array(orders_list, dtype=jnp.float32)
    angle_table = azimuth[:, None] * orders_row[None, :]
    cos_table = jnp.cos(angle_table)
    sin_table = jnp.sin(angle_table)
    scale_real = jnp.array(phase_real, dtype=jnp.float32)[None, :]
    scale_imag = jnp.array(phase_imag, dtype=jnp.float32)[None, :]
    wave_real = (scale_real * cos_table - scale_imag * sin_table)[None, :, :]
    wave_imag = (scale_real * sin_table + scale_imag * cos_table)[None, :, :]
    theta_real = jnp.concatenate([-pi_block * wave_imag, tau_block * wave_real], axis=-1)
    theta_imag = jnp.concatenate([pi_block * wave_real, tau_block * wave_imag], axis=-1)
    phi_real = jnp.concatenate([-tau_block * wave_real, -pi_block * wave_imag], axis=-1)
    phi_imag = jnp.concatenate([-tau_block * wave_imag, pi_block * wave_real], axis=-1)
    real_part = jnp.stack([theta_real, phi_real])
    imag_part = jnp.stack([theta_imag, phi_imag])
    return (real_part, imag_part, sine_theta)


def evaluate_far(real_part, imag_part, anchor):
    half = anchor.shape[1] // 2
    first = jnp.einsum("cikp,pf->cikf", real_part, anchor, precision=lax.Precision.HIGHEST)
    second = jnp.einsum("cikp,pf->cikf", imag_part, anchor, precision=lax.Precision.HIGHEST)
    real_out = first[..., :half] - second[..., half:]
    imag_out = first[..., half:] + second[..., :half]
    return jnp.stack([real_out, imag_out], axis=1)


def rotate_step(matrix, vector):
    product = jnp.einsum("sap,spf->saf", matrix, vector, preferred_element_type=jnp.float32)
    half_rows = matrix.shape[2]
    half_cols = vector.shape[2] // 2
    real_out = product[:, :half_rows, :half_cols] - product[:, half_rows:, half_cols:]
    imag_out = product[:, half_rows:, :half_cols] + product[:, :half_rows, half_cols:]
    return jnp.concatenate([real_out, imag_out], axis=2)


def shards(coefficients, positions, shift_tables, absorb_weight, incident, detector):
    fields = coefficients.shape[2] // 2
    coef_count = coefficients.shape[1]
    along_z = jnp.take(shift_tables[2], positions[:, 2], axis=0)
    along_y = jnp.take(shift_tables[1], positions[:, 1], axis=0)
    along_x = jnp.take(shift_tables[0], positions[:, 0], axis=0)
    first = rotate_step(along_z, coefficients).astype(jnp.bfloat16)
    second = rotate_step(along_y, first).astype(jnp.bfloat16)
    moved = rotate_step(along_x, second)
    partial_value = jnp.sum(moved, axis=0)
    widened = coefficients.astype(jnp.float32)
    squares = widened * widened
    energy = squares[:, :, :fields] + squares[:, :, fields:]
    absorbed = jnp.einsum("sp,spf->f", absorb_weight, energy)
    extinction = jnp.sum(
        incident[:, :fields] * partial_value[:, :fields]
        + incident[:, fields:] * partial_value[:, fields:],
        axis=0,
    )
    local_stats = jnp.stack([extinction, absorbed])
    partial_split = partial_value.reshape(coef_count, 2, fields)
    polar_total = POL_DEV * lax.axis_size("sph")
    polar_index = lax.axis_index("sph") * POL_DEV + jnp.arange(POL_DEV)
    groups = lax.axis_size("ang")
    share = fields // groups
    solid_angle = 2.0 * math.pi * math.pi / (polar_total * AZIM)
    anchor_split, stats = lax.psum((partial_split, local_stats), ("sph", "ang"))
    azim_share = AZIM // groups
    azim_start = lax.axis_index("ang") * azim_share
    azim_index = azim_start + jnp.arange(azim_share)
    real_part, imag_part, sine_theta = angular_basis(
        polar_index, azim_index, polar_total, AZIM, ORDER
    )
    amplitude = evaluate_far(real_part, imag_part, anchor_split.reshape(coef_count, 2 * fields))
    local_detector = lax.dynamic_slice_in_dim(detector, azim_start, azim_share, 1)
    weight = local_detector * sine_theta[:, None] * solid_angle
    power = jnp.einsum("crikf,ik->f", amplitude * amplitude, weight)
    collected = lax.psum_scatter(power, "ang", scatter_dimension=0, tiled=True)
    collected = lax.psum(collected, "sph")
    own_stats = lax.dynamic_slice_in_dim(stats, lax.axis_index("ang") * share, share, 1)
    cross_sections = jnp.concatenate([own_stats, collected[None, :]], axis=0)
    return (amplitude, cross_sections)


def solution(mesh):
    placed = (
        P(("sph", "ang"), None, None),
        P(("sph", "ang"), None),
        P(),
        P(("sph", "ang"), None),
        P(),
        P("sph", None),
    )
    return jax.shard_map(
        shards,
        mesh=mesh,
        in_specs=placed,
        out_specs=(P(None, None, "sph", "ang", None), P(None, "ang")),
        check_vma=False,
    )
```

profile of v0, /device:TPU:0, one launch (start us, length us, event | category | flops | bytes accessed | tf_op | source)
XLA Modules:
  0.0 254.2 jit_solution(17758391303258946681)
XLA Ops:
  7.2 5.3 %slice_bitcast_fusion.2 = (bf16[8,480,240]{2,1,0:T(8,128)(2,1)}, bf16[8,480,240]{2,1,0:T(8,128)(2,1)}, bf16[8,480,240]{2,1,0:T(8,128)(2,1)}) fusion(bf16[3,8,480,240]{3,2,1,0:T(8,128)(2,1)} %param.13), kind=kLoop, calls=%fused_computation.32 | loop fusion | bytes 11059200 | tf_op jit(solution)/shard_map/squeeze | solution.py:114
  12.6 2.2 gather_fusion.2
  14.8 9.8 %fusion.14 = f32[8,480,1024]{2,1,0:T(8,128)} fusion(bf16[8,240,1024]{2,1,0:T(8,128)(2,1)} %param.11, bf16[8,480,240]{2,1,0:T(8,128)(2,1)S(1)} %gather_fusion.2, pred[8]{0:T(512)(128)(4,1)S(1)} %get-tuple-element.41), kind=kOutput, calls=%fused_computation.26 | convolution fusion | flops 1888358400 | bytes 21504008 | tf_op jit(solution)/shard_map/sap,spf->saf/dot_general | solution.py:101
  24.6 9.0 %fusion.5 = (bf16[8,240,512]{2,1,0:T(8,128)(2,1)}, bf16[8,240,512]{2,1,0:T(8,128)(2,1)}) fusion(f32[8,480,1024]{2,1,0:T(8,128)} %fusion.14), kind=kLoop, calls=%fused_computation.17 | loop fusion | flops 3932160 | bytes 19660800 | tf_op jit(solution)/shard_map/convert.2
  33.6 2.2 gather_fusion.1
  35.9 9.8 %fusion.6 = f32[8,480,1024]{2,1,0:T(8,128)} fusion(bf16[8,240,512]{2,1,0:T(8,128)(2,1)} %get-tuple-element.18, bf16[8,240,512]{2,1,0:T(8,128)(2,1)} %get-tuple-element.17, bf16[8,480,240]{2,1,0:T(8,128)(2,1)S(1)} %gather_fusion.1, pred[8]{0:T(512)(128)(4,1)S(1)} %get-tuple-element.43), kind=kOutput, calls=%fused_computation.18 | convolution fusion | flops 1896222720 | bytes 21504008 | tf_op jit(solution)/shard_map/sap,spf->saf/dot_general | solution.py:101
  45.7 9.1 %fusion.3 = (bf16[8,240,512]{2,1,0:T(8,128)(2,1)}, bf16[8,240,512]{2,1,0:T(8,128)(2,1)}) fusion(f32[8,480,1024]{2,1,0:T(8,128)} %fusion.6), kind=kLoop, calls=%fused_computation.13 | loop fusion | flops 3932160 | bytes 19660800 | tf_op jit(solution)/shard_map/convert
  54.8 2.2 gather_fusion
  57.0 9.8 %fusion.10 = f32[8,480,1024]{2,1,0:T(8,128)} fusion(bf16[8,240,512]{2,1,0:T(8,128)(2,1)} %get-tuple-element.16, bf16[8,240,512]{2,1,0:T(8,128)(2,1)} %get-tuple-element.15, bf16[8,480,240]{2,1,0:T(8,128)(2,1)S(1)} %gather_fusion, pred[8]{0:T(512)(128)(4,1)S(1)} %get-tuple-element.7), kind=kOutput, calls=%fused_computation.22 | convolution fusion | flops 1896222720 | bytes 21504008 | tf_op jit(solution)/shard_map/sap,spf->saf/dot_general | solution.py:101
  66.8 7.8 %slice_subtract_fusion = (f32[8,240,512]{2,1,0:T(8,128)S(1)}, f32[8,240,512]{2,1,0:T(8,128)S(1)}) fusion(f32[8,480,1024]{2,1,0:T(8,128)} %fusion.10), kind=kLoop, calls=%fused_computation.9 | loop fusion | flops 1966080 | bytes 23592960 | tf_op jit(solution)/shard_map/sub | solution.py:104
  74.6 0.9 maximum_reduce_fusion
  75.5 0.3 copy-done.2
  75.8 0.2 fusion.30
  76.1 0.4 copy-done.1
  76.5 0.3 all-reduce.3.cloned.1.call-update
  78.1 0.1 fusion.53
  78.5 0.1 multiply_divide_fusion.70
  78.9 0.1 multiply_divide_fusion.56
  79.0 0.1 multiply_divide_fusion.54
  79.1 0.1 fusion.51
  79.5 0.1 multiply_divide_fusion.42
  79.5 0.1 multiply_divide_fusion.40
  79.6 0.1 multiply_divide_fusion.38
  79.7 0.1 multiply_divide_fusion.36
  80.1 0.1 multiply_divide_fusion.24
  80.1 0.1 multiply_divide_fusion.22
  80.2 0.1 multiply_divide_fusion.20
  80.3 0.1 multiply_divide_fusion.18
  80.4 0.1 fusion.49
  80.5 0.1 multiply_divide_fusion.16
  80.5 0.1 multiply_divide_fusion.14
  80.7 0.1 fusion.46
  81.5 0.1 subtract_divide_fusion.35
  81.6 0.1 multiply_divide_fusion.5
  81.8 0.1 subtract_divide_fusion.28
  81.8 0.1 multiply_divide_fusion.4
  82.1 0.1 subtract_divide_fusion.21
  82.1 0.1 subtract_divide_fusion.19
  82.3 0.1 subtract_divide_fusion.14
  82.4 0.1 subtract_divide_fusion.12
  82.5 0.1 subtract_divide_fusion.10
  82.7 0.1 subtract_divide_fusion.5
  82.8 0.1 subtract_divide_fusion.3
  82.8 0.1 subtract_divide_fusion.1
  82.9 6.4 %convert_multiply_fusion = f32[8,240,1024]{2,1,0:T(8,128)} fusion(bf16[8,240,1024]{2,1,0:T(8,128)(2,1)} %param.11), kind=kLoop, calls=%fused_computation.4 | loop fusion | flops 3932160 | bytes 11796480 | tf_op jit(solution)/shard_map/mul | solution.py:120
  89.4 0.2 stack.28
  89.6 0.2 stack.29
  89.9 3.8 %fusion.21 = f32[1,512]{1,0:T(1,128)S(1)} fusion(f32[8,240,1024]{2,1,0:T(8,128)} %convert_multiply_fusion, f32[8,240,1]{1,0,2:T(8,128)S(1)} %bitcast.50), kind=kOutput, calls=%fused_computation.36 | convolution fusion | flops 2949120 | bytes 7874048 | tf_op jit(solution)/shard_map/sp,spf->f/dot_general | solution.py:122
  93.7 42.0 %psum.22 = f32[2,512]{1,0:T(2,128)S(1)} all-reduce(f32[2,512]{1,0:T(2,128)S(1)} %pad_maximum_fusion.1), channel_id=1, replica_groups=mesh['sph'=8,'ang'=4] {'sph','ang'}, use_global_device_ids=true, to_apply=%region_3.5 | all-reduce | flops 1024 | bytes 8192 | tf_op jit(solution)/shard_map/psum | solution.py:135
  135.7 0.1 fusion.43
  135.9 0.6 dynamic-slice
  137.1 0.1 maximum_bitcast_fusion.2
  137.2 0.1 maximum_bitcast_fusion
  137.3 0.1 multiply_multiply_fusion.4
  137.4 76.9 %all-reduce.3.cloned.1.call-done = f32[240,1024]{1,0:T(8,128)} async-done(((f32[240,1024]{1,0:T(8,128)}), f32[240,1024]{1,0:T(8,128)}) %all-reduce.3.cloned.1.call-update) | async-done | bytes 983056 | tf_op jit(solution)/shard_map/psum | solution.py:135
  214.3 1.9 fusion.22
  216.2 1.9 fusion.24
  218.1 0.1 fusion.32
  218.2 0.8 copy.12
  219.1 0.2 fusion.78
  219.3 6.8 %all-reduce = f32[512]{0:T(512)S(1)} all-reduce(f32[512]{0:T(512)S(1)} %bitcast.53), channel_id=2, replica_groups=mesh['sph'=8,'ang'=4] {'ang'}, use_global_device_ids=true, to_apply=%region_5.7.clone | all-reduce | flops 512 | bytes 4096
  226.1 0.1 dynamic-slice_bitcast_fusion
  226.2 20.6 %psum.23 = f32[1,128]{1,0:T(1,128)S(1)} all-reduce(f32[1,128]{1,0:T(1,128)S(1)} %dynamic-slice_bitcast_fusion), channel_id=1, replica_groups=mesh['sph'=8,'ang'=4] {'sph'}, use_global_device_ids=true, to_apply=%region_6.8 | all-reduce | flops 128 | bytes 1024 | tf_op jit(solution)/shard_map/psum | solution.py:147
  246.8 0.6 pad_maximum_fusion.2
  (92 shorter events, 4.0 us)
Async XLA Ops:
  7.2 82.7 %copy-start = (f32[8,240]{1,0:T(8,128)S(1)}, f32[8,240]{1,0:T(8,128)}, u32[]{:S(2)}) copy-start(f32[8,240]{1,0:T(8,128)} %param.14) | copy-start | bytes 23044
  7.2 5.4 %copy-start.4 = (s32[8,3]{0,1:T(4,128)S(1)}, s32[8,3]{0,1:T(4,128)}, u32[]{:S(2)}) copy-start(s32[8,3]{0,1:T(4,128)} %param.12) | copy-start | bytes 292
  74.6 1.2 copy-start.2
  75.5 0.9 copy-start.1
  76.0 138.2 %all-reduce.3.cloned.1.call-start = ((), (), s32[]{:S(2)}) async-start(), calls=%async_computation | async-start | bytes 1966080 | tf_op jit(solution)/shard_map/psum | solution.py:135
  89.3 46.3 %copy-start.5 = (f32[120]{0:T(128)S(1)}, f32[120]{0:T(128)}, u32[]{:S(2)}) copy-start(f32[120]{0:T(128)} %constant.609.clone) | copy-start | bytes 1444
  89.3 46.3 %copy-start.6 = (f32[120]{0:T(128)S(1)}, f32[120]{0:T(128)}, u32[]{:S(2)}) copy-start(f32[120]{0:T(128)} %constant.607.clone) | copy-start | bytes 1444
  89.3 46.3 %copy-start.7 = (f32[120]{0:T(128)S(1)}, f32[120]{0:T(128)}, u32[]{:S(2)}) copy-start(f32[120]{0:T(128)} %constant.608.clone) | copy-start | bytes 1444
  89.3 46.5 %copy-start.8 = (u32[32]{0:T(128)S(1)}, u32[32]{0:T(128)}, u32[]{:S(2)}) copy-start(u32[32]{0:T(128)} %constant.616) | copy-start | bytes 388
  89.3 48.0 %copy-start.3 = (f32[4,64]{1,0:T(4,128)S(1)}, f32[4,64]{1,0:T(4,128)}, u32[]{:S(2)}) copy-start(f32[4,64]{1,0:T(4,128)} %param.16) | copy-start | bytes 3076
Sparse Core Ops, SparseCore 0:
  82.0 132.1 all-reduce.2
where the time goes:
time: 255 us; the launch traced here: 254 us
  waiting for transfers between devices  77.1 us (30%)
  blocking collectives  69.4 us (27%)
  other arithmetic  40.4 us (16%)
  matrix products  37.2 us (15%)
  between operations  15.3 us (6%)
  local copies, waits for them, and re-layouts  14.7 us (6%)
    psum x1, waiting for transfers between devices, shards(): anchor_split, stats = lax.psum((partial_split, local_stats), ('sph', 'ang'))  76.9 us
    psum x1, blocking collectives, shards(): anchor_split, stats = lax.psum((partial_split, local_stats), ('sph', 'ang'))  42 us
    dot_general x3, matrix products, rotate_step(): jnp.einsum('sap,spf->saf', matrix, vector, preferred_element_type=jnp.flo...  29.4 us
    psum x1, blocking collectives, shards(): collected = lax.psum(collected, 'sph')  20.6 us
    another operation x2, other arithmetic  18.1 us
    sub x1, other arithmetic, rotate_step(): product[:, :half_rows, :half_cols] - product[:, half_rows:, half_cols:]  7.76 us
    unnamed x1, blocking collectives  6.84 us
    mul x1, other arithmetic, shards(): squares = widened * widened  6.4 us
  transfers between devices with their start and end apart: 1, of which 1 were waited for; matrix products, arithmetic and copies ran while one was open for 7% of the time, Pallas kernels for 0%

commit v1 on v0

--- a/solution.py
+++ b/solution.py
@@ -144,7 +144,11 @@
     weight = local_detector * sine_theta[:, None] * solid_angle
     power = jnp.einsum("crikf,ik->f", amplitude * amplitude, weight)
     collected = lax.psum_scatter(power, "ang", scatter_dimension=0, tiled=True)
-    collected = lax.psum(collected, "sph")
+    size, total = (lax.axis_size("sph"), collected)
+    for hop in [1 << k for k in range(size.bit_length() - 1)]:
+        swap = [(i, i ^ hop) for i in range(size)]
+        total = total + lax.ppermute(total, "sph", swap)
+    collected = total
     own_stats = lax.dynamic_slice_in_dim(stats, lax.axis_index("ang") * share, share, 1)
     cross_sections = jnp.concatenate([own_stats, collected[None, :]], axis=0)
     return (amplitude, cross_sections)

time: 255 us -> 281 us (1.10)
  waiting for transfers between devices: 77.1 us -> 123 us
  blocking collectives: 69.4 us -> 45.1 us
  starting transfers between devices: 0.04 us -> 4.63 us
    psum x1, waiting for transfers between devices: 76.9 us -> 119 us  [shards(): anchor_split, stats = lax.psum((partial_split, local_stats), ('sph', 'ang'))]
    psum x1 -> x0, blocking collectives: 20.6 us -> none  [shards(): collected = lax.psum(collected, 'sph')]
    ppermute x0 -> x3, starting transfers between devices: none -> 4.59 us  [shards(): total = total + lax.ppermute(total, 'sph', swap)]
    ppermute x0 -> x3, waiting for transfers between devices: none -> 4.09 us  [shards(): total = total + lax.ppermute(total, 'sph', swap)]
    psum x1, blocking collectives: 42 us -> 38.2 us  [shards(): anchor_split, stats = lax.psum((partial_split, local_stats), ('sph', 'ang'))]
  transfers between devices with their start and end apart: 1 -> 4, of which waited for: 1 -> 3; matrix products, arithmetic and copies ran while one was open for 7% -> 7% of each run, Pallas kernels for 0% -> 0%
where the time goes in v1:
time: 281 us
  waiting for transfers between devices  123 us (44%)
  blocking collectives  45.1 us (16%)
  other arithmetic  40.5 us (14%)
  matrix products  37.3 us (13%)
  between operations  15.3 us (5%)
  local copies, waits for them, and re-layouts  14.8 us (5%)
  starting transfers between devices  4.63 us (2%)
    psum x1, waiting for transfers between devices, shards(): anchor_split, stats = lax.psum((partial_split, local_stats), ('sph', 'ang'))  119 us
    psum x1, blocking collectives, shards(): anchor_split, stats = lax.psum((partial_split, local_stats), ('sph', 'ang'))  38.2 us
    dot_general x3, matrix products, rotate_step(): jnp.einsum('sap,spf->saf', matrix, vector, preferred_element_type=jnp.flo...  29.5 us
    another operation x2, other arithmetic  18.1 us
    sub x1, other arithmetic, rotate_step(): product[:, :half_rows, :half_cols] - product[:, half_rows:, half_cols:]  7.76 us
    unnamed x1, blocking collectives  6.84 us
    mul x1, other arithmetic, shards(): squares = widened * widened  6.4 us
  transfers between devices with their start and end apart: 4, of which 3 were waited for; matrix products, arithmetic and copies ran while one was open for 7% of the time, Pallas kernels for 0%

profile of v1, /device:TPU:0, one launch (start us, length us, event | category | flops | bytes accessed | tf_op | source)
XLA Modules:
  0.0 280.8 jit_solution(11473759385775794574)
XLA Ops:
  7.2 5.4 %slice_bitcast_fusion.2 = (bf16[8,480,240]{2,1,0:T(8,128)(2,1)}, bf16[8,480,240]{2,1,0:T(8,128)(2,1)}, bf16[8,480,240]{2,1,0:T(8,128)(2,1)}) fusion(bf16[3,8,480,240]{3,2,1,0:T(8,128)(2,1)} %param.13), kind=kLoop, calls=%fused_computation.32 | loop fusion | bytes 11059200 | tf_op jit(solution)/shard_map/squeeze | solution.py:114
  12.6 2.2 gather_fusion.2
  14.8 9.8 %fusion.14 = f32[8,480,1024]{2,1,0:T(8,128)} fusion(bf16[8,240,1024]{2,1,0:T(8,128)(2,1)} %param.11, bf16[8,480,240]{2,1,0:T(8,128)(2,1)S(1)} %gather_fusion.2, pred[8]{0:T(512)(128)(4,1)S(1)} %get-tuple-element.41), kind=kOutput, calls=%fused_computation.26 | convolution fusion | flops 1888358400 | bytes 21504008 | tf_op jit(solution)/shard_map/sap,spf->saf/dot_general | solution.py:101
  24.6 9.0 %fusion.5 = (bf16[8,240,512]{2,1,0:T(8,128)(2,1)}, bf16[8,240,512]{2,1,0:T(8,128)(2,1)}) fusion(f32[8,480,1024]{2,1,0:T(8,128)} %fusion.14), kind=kLoop, calls=%fused_computation.17 | loop fusion | flops 3932160 | bytes 19660800 | tf_op jit(solution)/shard_map/convert.2
  33.7 2.2 gather_fusion.1
  35.9 9.9 %fusion.6 = f32[8,480,1024]{2,1,0:T(8,128)} fusion(bf16[8,240,512]{2,1,0:T(8,128)(2,1)} %get-tuple-element.18, bf16[8,240,512]{2,1,0:T(8,128)(2,1)} %get-tuple-element.17, bf16[8,480,240]{2,1,0:T(8,128)(2,1)S(1)} %gather_fusion.1, pred[8]{0:T(512)(128)(4,1)S(1)} %get-tuple-element.43), kind=kOutput, calls=%fused_computation.18 | convolution fusion | flops 1896222720 | bytes 21504008 | tf_op jit(solution)/shard_map/sap,spf->saf/dot_general | solution.py:101
  45.8 9.1 %fusion.3 = (bf16[8,240,512]{2,1,0:T(8,128)(2,1)}, bf16[8,240,512]{2,1,0:T(8,128)(2,1)}) fusion(f32[8,480,1024]{2,1,0:T(8,128)} %fusion.6), kind=kLoop, calls=%fused_computation.13 | loop fusion | flops 3932160 | bytes 19660800 | tf_op jit(solution)/shard_map/convert
  54.9 2.2 gather_fusion
  57.1 9.9 %fusion.10 = f32[8,480,1024]{2,1,0:T(8,128)} fusion(bf16[8,240,512]{2,1,0:T(8,128)(2,1)} %get-tuple-element.16, bf16[8,240,512]{2,1,0:T(8,128)(2,1)} %get-tuple-element.15, bf16[8,480,240]{2,1,0:T(8,128)(2,1)S(1)} %gather_fusion, pred[8]{0:T(512)(128)(4,1)S(1)} %get-tuple-element.7), kind=kOutput, calls=%fused_computation.22 | convolution fusion | flops 1896222720 | bytes 21504008 | tf_op jit(solution)/shard_map/sap,spf->saf/dot_general | solution.py:101
  66.9 7.8 %slice_subtract_fusion = (f32[8,240,512]{2,1,0:T(8,128)S(1)}, f32[8,240,512]{2,1,0:T(8,128)S(1)}) fusion(f32[8,480,1024]{2,1,0:T(8,128)} %fusion.10), kind=kLoop, calls=%fused_computation.9 | loop fusion | flops 1966080 | bytes 23592960 | tf_op jit(solution)/shard_map/sub | solution.py:104
  74.7 0.9 maximum_reduce_fusion
  75.6 0.3 copy-done.2
  75.9 0.2 fusion.30
  76.2 0.4 copy-done.1
  76.6 0.3 all-reduce.3.cloned.1.call-update
  78.6 0.1 multiply_divide_fusion.70
  79.0 0.1 multiply_divide_fusion.56
  79.1 0.1 multiply_divide_fusion.54
  79.2 0.1 fusion.51
  79.6 0.1 multiply_divide_fusion.40
  79.7 0.1 multiply_divide_fusion.38
  79.8 0.1 multiply_divide_fusion.36
  80.2 0.1 multiply_divide_fusion.22
  80.3 0.1 multiply_divide_fusion.20
  80.4 0.1 multiply_divide_fusion.18
  80.5 0.1 fusion.49
  80.6 0.1 multiply_divide_fusion.16
  80.8 0.1 fusion.46
  81.7 0.1 multiply_divide_fusion.5
  81.9 0.1 subtract_divide_fusion.28
  82.0 0.1 multiply_divide_fusion.4
  82.2 0.1 subtract_divide_fusion.21
  82.2 0.1 subtract_divide_fusion.19
  82.4 0.1 subtract_divide_fusion.14
  82.5 0.1 subtract_divide_fusion.12
  82.6 0.1 subtract_divide_fusion.10
  82.8 0.1 subtract_divide_fusion.5
  82.9 0.1 subtract_divide_fusion.3
  82.9 0.1 subtract_divide_fusion.1
  83.1 6.4 %convert_multiply_fusion = f32[8,240,1024]{2,1,0:T(8,128)} fusion(bf16[8,240,1024]{2,1,0:T(8,128)(2,1)} %param.11), kind=kLoop, calls=%fused_computation.4 | loop fusion | flops 3932160 | bytes 11796480 | tf_op jit(solution)/shard_map/mul | solution.py:120
  89.5 0.2 stack.28
  89.8 0.2 stack.29
  90.1 0.6 dynamic-slice
  91.3 0.1 fusion.43
  91.5 0.1 maximum_bitcast_fusion.2
  91.6 0.1 maximum_bitcast_fusion
  91.7 0.1 multiply_multiply_fusion.4
  91.8 3.8 %fusion.21 = f32[1,512]{1,0:T(1,128)S(1)} fusion(f32[8,240,1024]{2,1,0:T(8,128)} %convert_multiply_fusion, f32[8,240,1]{1,0,2:T(8,128)S(1)} %bitcast.50), kind=kOutput, calls=%fused_computation.36 | convolution fusion | flops 2949120 | bytes 7874048 | tf_op jit(solution)/shard_map/sp,spf->f/dot_general | solution.py:122
  95.6 118.9 %all-reduce.3.cloned.1.call-done = f32[240,1024]{1,0:T(8,128)} async-done(((f32[240,1024]{1,0:T(8,128)}), f32[240,1024]{1,0:T(8,128)}) %all-reduce.3.cloned.1.call-update) | async-done | bytes 983056 | tf_op jit(solution)/shard_map/psum | solution.py:135
  214.5 1.9 fusion.22
  216.4 1.9 fusion.24
  218.3 0.1 fusion.32
  218.5 0.2 fusion.78
  218.6 6.8 %all-reduce = f32[512]{0:T(512)S(1)} all-reduce(f32[512]{0:T(512)S(1)} %bitcast.53), channel_id=2, replica_groups=mesh['sph'=8,'ang'=4] {'ang'}, use_global_device_ids=true, to_apply=%region_5.7.clone | all-reduce | flops 512 | bytes 4096
  225.5 0.1 dynamic-slice.1
  225.6 0.6 collective-permute-start
  226.1 3.0 %collective-permute-done = f32[128]{0:T(128)S(1)} collective-permute-done((f32[128]{0:T(128)S(1)}, f32[128]{0:T(128)S(1)}, u32[]{:S(2)}, u32[]{:S(2)}) %collective-permute-start) | collective-permute-done | bytes 544 | tf_op jit(solution)/shard_map/ppermute | solution.py:150
  229.1 0.1 dynamic-slice_add_fusion
  229.2 1.4 collective-permute-start.1
  230.6 38.2 %psum.15 = f32[2,512]{1,0:T(2,128)S(1)} all-reduce(f32[2,512]{1,0:T(2,128)S(1)} %pad_maximum_fusion.1), channel_id=1, replica_groups=mesh['sph'=8,'ang'=4] {'sph','ang'}, use_global_device_ids=true, to_apply=%region_3.5 | all-reduce | flops 1024 | bytes 8192 | tf_op jit(solution)/shard_map/psum | solution.py:135
  268.9 2.6 collective-permute-start.2
  271.5 0.8 copy.12
  272.3 1.1 collective-permute-done.2
  273.4 0.6 pad_maximum_fusion.2
  (100 shorter events, 4.3 us)
Async XLA Ops:
  7.2 84.6 %copy-start = (f32[8,240]{1,0:T(8,128)S(1)}, f32[8,240]{1,0:T(8,128)}, u32[]{:S(2)}) copy-start(f32[8,240]{1,0:T(8,128)} %param.14) | copy-start | bytes 23044
  7.2 5.4 %copy-start.4 = (s32[8,3]{0,1:T(4,128)S(1)}, s32[8,3]{0,1:T(4,128)}, u32[]{:S(2)}) copy-start(s32[8,3]{0,1:T(4,128)} %param.12) | copy-start | bytes 292
  74.7 1.2 copy-start.2
  75.6 1.0 copy-start.1
  76.1 138.4 %all-reduce.3.cloned.1.call-start = ((), (), s32[]{:S(2)}) async-start(), calls=%async_computation | async-start | bytes 1966080 | tf_op jit(solution)/shard_map/psum | solution.py:135
  83.1 7.0 %copy-start.8 = (u32[32]{0:T(128)S(1)}, u32[32]{0:T(128)}, u32[]{:S(2)}) copy-start(u32[32]{0:T(128)} %constant.616) | copy-start | bytes 388
  83.1 8.2 %copy-start.5 = (f32[120]{0:T(128)S(1)}, f32[120]{0:T(128)}, u32[]{:S(2)}) copy-start(f32[120]{0:T(128)} %constant.609.clone) | copy-start | bytes 1444
  83.1 8.2 %copy-start.6 = (f32[120]{0:T(128)S(1)}, f32[120]{0:T(128)}, u32[]{:S(2)}) copy-start(f32[120]{0:T(128)} %constant.607.clone) | copy-start | bytes 1444
  83.1 8.2 %copy-start.7 = (f32[120]{0:T(128)S(1)}, f32[120]{0:T(128)}, u32[]{:S(2)}) copy-start(f32[120]{0:T(128)} %constant.608.clone) | copy-start | bytes 1444
  83.1 8.6 %copy-start.3 = (f32[4,64]{1,0:T(4,128)S(1)}, f32[4,64]{1,0:T(4,128)}, u32[]{:S(2)}) copy-start(f32[4,64]{1,0:T(4,128)} %param.16) | copy-start | bytes 3076
  225.6 3.6 %collective-permute-start = (f32[128]{0:T(128)S(1)}, f32[128]{0:T(128)S(1)}, u32[]{:S(2)}, u32[]{:S(2)}) collective-permute-start(f32[128]{0:T(128)S(1)} %dynamic-slice.1), channel_id=1, source_target_pairs={{0,4},{4,0},{8,12},{12,8},{16,20},{20,16},{24,28},{28,24},{1,5},{5... | collective-permute-start | bytes 1544 | tf_op jit(solution)/shard_map/ppermute | solution.py:150
  229.2 39.7 %collective-permute-start.1 = (f32[128]{0:T(128)S(1)}, f32[128]{0:T(128)S(1)}, u32[]{:S(2)}, u32[]{:S(2)}) collective-permute-start(f32[128]{0:T(128)S(1)} %dynamic-slice_add_fusion), channel_id=1, source_target_pairs={{0,8},{4,12},{8,0},{12,4},{16,24},{20,28},{24,16},{28,20},{1,9},{5... | collective-permute-start | bytes 1544 | tf_op jit(solution)/shard_map/ppermute | solution.py:150
  268.9 4.5 %collective-permute-start.2 = (f32[128]{0:T(128)S(1)}, f32[128]{0:T(128)S(1)}, u32[]{:S(2)}, u32[]{:S(2)}) collective-permute-start(f32[128]{0:T(128)S(1)} %add.2556), channel_id=1, source_target_pairs={{0,16},{4,20},{8,24},{12,28},{16,0},{20,4},{24,8},{28,12},{1,17},{... | collective-permute-start | bytes 1544 | tf_op jit(solution)/shard_map/ppermute | solution.py:150
Sparse Core Ops, SparseCore 0:
  82.1 132.3 all-reduce.2
